TPU v7x, 32 devices: a whole 2x2x4 slice. The times are simulated.
32 devices in a mesh: chan: 4 (over y, x), hid: 8 (over z, core).
Axes of the slice: x: 2, y: 2, z: 4, core: 2. Of those that a mesh axis runs over, the one named last changes fastest.
Arguments:
- pixels: bfloat16 [384, 256, 256], P('chan'), may hold values from -6 to 6
- patch_weight: bfloat16 [384, 256, 6144], P('chan', None, 'hid'), may hold values from -0.375 to 0.375
- channel_embed: bfloat16 [384, 6144], P('chan', 'hid'), may hold values from -3 to 3
- pool_query: bfloat16 [48, 6144], P('chan', 'hid'), may hold values from -2.5 to 2.5
- group_mix: bfloat16 [48, 6144], P('chan', 'hid'), may hold values from -3.2 to 3.2
- assign: int32 [384], P('chan'), may hold values from 0 to 47, as said below
- ln_gain: float32 [6144], P('chan'), may hold values from 0.1 to 1.9
- w_qkv: bfloat16 [6144, 3, 6144], P('chan', None, 'hid'), may hold values from -0.078125 to 0.078125
- w_up: bfloat16 [6144, 24576], P('chan', 'hid'), may hold values from -0.078125 to 0.078125
- b_up: float32 [24576], P('hid'), may hold values from -3 to 3
- w_out: bfloat16 [6144, 6144], P('hid', 'chan'), may hold values from -0.078125 to 0.078125
- w_down: bfloat16 [24576, 6144], P('hid', 'chan'), may hold values from -0.0390625 to 0.0390625
Outputs:
- block_out: bfloat16 [256, 6144], P(None, 'chan')
Inputs may be any that keep to these rules, and one draw needn't show every extreme that they name: Channel c belongs to group assign[c]; every group holds exactly 8 channels, and group k's channels all lie among the 96 consecutive channels beginning at channel (k // 12) * 96.
All inputs are finite; a program needn't handle non-finite values.
Results may differ from a plain program's by a relative error of at most 0.02.
Values may be sent and summed in bfloat16 or wider, within the bound.
A program may use at most 320 MiB of HBM per device.

v0:
```python
import math
import jax
import jax.numpy as jnp
from jax import lax
from jax.sharding import PartitionSpec as P

HS = 128
PATCHES = 256
D = 6144
epsilon = 1e-06


def head_norm(values):
    return values * lax.rsqrt(jnp.mean(values * values, axis=-1, keepdims=True) + epsilon)


def finish_rows(qkv_rows, up_rows, b_up, heads_dev):
    rows = qkv_rows.shape[0]
    width = heads_dev * HS
    query_part = (
        head_norm(qkv_rows[:, 0].reshape(rows, heads_dev, HS))
        .astype(jnp.bfloat16)
        .reshape(rows, width)
    )
    key_part = (
        head_norm(qkv_rows[:, 1].reshape(rows, heads_dev, HS))
        .astype(jnp.bfloat16)
        .reshape(rows, width)
    )
    value_part = qkv_rows[:, 2].astype(jnp.bfloat16)
    hidden_part = jax.nn.gelu(up_rows + b_up, approximate=False).astype(jnp.bfloat16)
    return (query_part, key_part, value_part, hidden_part)


def on_device(
    pixels,
    patch_weight,
    channel_embed,
    pool_query,
    group_mix,
    assign,
    ln_gain,
    w_qkv,
    w_up,
    b_up,
    w_out,
    w_down,
):
    chan_count = pixels.shape[0]
    tok_count = pixels.shape[1]
    width_hid = patch_weight.shape[2]
    width_chan = ln_gain.shape[0]
    heads_dev = width_hid // HS
    groups_dev = pool_query.shape[0]
    embedded = jnp.einsum("ctp,cpd->ctd", pixels, patch_weight, preferred_element_type=jnp.float32)
    embedded = embedded + channel_embed.astype(jnp.float32)[:, None, :]
    features = jax.nn.gelu(embedded, approximate=False)
    split = features.reshape(chan_count, tok_count, heads_dev, HS)
    normed = head_norm(split)
    local_group = assign - lax.axis_index("chan") * groups_dev
    member = (local_group[None, :] == jnp.arange(groups_dev, dtype=jnp.int32)[:, None]).astype(
        jnp.float32
    )
    query = jnp.dot(member.T, pool_query.astype(jnp.float32), precision=lax.Precision.HIGHEST)
    query = query.reshape(chan_count, heads_dev, HS)
    score = jnp.einsum("cthe,che->cth", normed, query, precision=lax.Precision.HIGHEST) / math.sqrt(
        HS
    )
    shift = jnp.sqrt(jnp.sum(query * query, axis=-1))
    weight = jnp.exp(score - shift[:, None, :])
    numer = jnp.einsum(
        "kc,cthe->kthe", member, weight[..., None] * split, precision=lax.Precision.HIGHEST
    )
    denom = jnp.einsum("kc,cth->kth", member, weight, precision=lax.Precision.HIGHEST)
    pooled = (numer / denom[..., None]).reshape(groups_dev, tok_count, width_hid)
    partial_value = jnp.einsum(
        "kd,ktd->td", group_mix.astype(jnp.float32), pooled, precision=lax.Precision.HIGHEST
    )
    layer_sum = lax.psum(partial_value.astype(jnp.bfloat16), "chan")
    gathered = lax.all_gather(layer_sum, "hid", axis=1, tiled=True)
    wide = gathered.astype(jnp.float32)
    row_total = jnp.sum(wide, axis=1)
    row_square = jnp.sum(wide * wide, axis=1)
    mine = lax.dynamic_slice_in_dim(gathered, lax.axis_index("chan") * width_chan, width_chan, 1)
    row_mean = row_total / D
    row_var = row_square / D - row_mean * row_mean
    own_cols = mine.astype(jnp.float32)
    normed_input = (
        (own_cols - row_mean[:, None]) * lax.rsqrt(row_var + epsilon)[:, None] * ln_gain
    ).astype(jnp.bfloat16)
    qkv_part = jnp.einsum("td,dke->tke", normed_input, w_qkv, preferred_element_type=jnp.float32)
    up_part = jnp.dot(normed_input, w_up, preferred_element_type=jnp.float32)
    qkv_share, up_share = (
        lax.psum_scatter(
            qkv_part.astype(jnp.bfloat16), "chan", scatter_dimension=0, tiled=True
        ).astype(jnp.float32),
        lax.psum_scatter(
            up_part.astype(jnp.bfloat16), "chan", scatter_dimension=0, tiled=True
        ).astype(jnp.float32),
    )
    query_share, key_share, value_share, hidden_share = finish_rows(
        qkv_share, up_share, b_up, heads_dev
    )
    query_rows, key_rows, value_rows, hidden = (
        lax.all_gather(query_share, "chan", axis=0, tiled=True),
        lax.all_gather(key_share, "chan", axis=0, tiled=True),
        lax.all_gather(value_share, "chan", axis=0, tiled=True),
        lax.all_gather(hidden_share, "chan", axis=0, tiled=True),
    )
    images = tok_count // PATCHES
    queries = query_rows.reshape(images, PATCHES, heads_dev, HS)
    keys = key_rows.reshape(images, PATCHES, heads_dev, HS)
    values = value_rows.reshape(images, PATCHES, heads_dev, HS)
    scores = jnp.einsum("bqhe,bkhe->bhqk", queries, keys, preferred_element_type=jnp.float32) * (
        2.0 / math.sqrt(HS)
    )
    expo = jnp.exp(scores)
    probs = (expo / jnp.sum(expo, axis=-1, keepdims=True)).astype(jnp.bfloat16)
    attended = jnp.einsum("bhqk,bkhe->bqhe", probs, values, preferred_element_type=jnp.float32)
    attended = attended.astype(jnp.bfloat16).reshape(tok_count, width_hid)
    term = jnp.dot(attended, w_out, preferred_element_type=jnp.float32) + jnp.dot(
        hidden, w_down, preferred_element_type=jnp.float32
    )
    mixed = lax.psum(term, "hid")
    return (own_cols + mixed).astype(jnp.bfloat16)


def solution(mesh):
    in_specs = (
        P("chan", None, None),
        P("chan", None, "hid"),
        P("chan", "hid"),
        P("chan", "hid"),
        P("chan", "hid"),
        P("chan"),
        P("chan"),
        P("chan", None, "hid"),
        P("chan", "hid"),
        P("hid"),
        P("hid", "chan"),
        P("hid", "chan"),
    )
    out_specs = P(None, "chan")
    return jax.shard_map(
        on_device, mesh=mesh, in_specs=in_specs, out_specs=out_specs, check_vma=False
    )
```

profile of v0, /device:TPU:0, one launch (start us, length us, event | category | flops | bytes accessed | tf_op | source)
XLA Modules:
  0.0 780.2 jit_solution(2045412981143405703)
XLA Ops:
  11.8 171.0 %fusion.1 = f32[96,256,768]{2,1,0:T(8,128)} fusion(f32[96,768]{1,0:T(8,128)S(1)} %convert_element_type.64, bf16[96,256,256]{2,1,0:T(8,128)(2,1)} %param.12, bf16[96,256,768]{2,1,0:T(8,128)(2,1)} %param.13), kind=kOutput, calls=%fused_computation.2 | convolution fusion | flops 10890510336 | bytes 126124032 | tf_op jit(solution)/shard_map/ctp,cpd->ctd/dot_general | solution.py:55
  182.8 72.9 %copy.57 = f32[96,256,768]{1,2,0:T(8,128)} copy(f32[96,256,768]{2,1,0:T(8,128)} %fusion.1) | data formatting | bytes 150994944 | tf_op jit(solution)/shard_map/mul | solution.py:57
  255.7 23.3 %multiply_reduce_fusion = f32[96,256,6]{1,2,0:T(8,128)S(1)} fusion(f32[96,256,6,128]{1,3,2,0:T(8,128)} %bitcast.4), kind=kLoop, calls=%fused_computation.5 | loop fusion | flops 37601280 | bytes 76087296 | tf_op jit(solution)/shard_map/reduce_sum | solution.py:14
  279.1 43.4 %fusion.2 = f32[96,6,1,256]{3,2,1,0:T(1,128)S(1)} fusion(f32[96,6,128,1]{2,3,1,0:T(1,128)S(1)} %copy-done.1, f32[96,256,6,128]{1,3,2,0:T(8,128)} %bitcast.4, f32[96,256,6]{1,2,0:T(8,128)S(1)} %add_rsqrt_fusion), kind=kOutput, calls=%fused_computation.3 | convolution fusion | flops 245366784 | bytes 76972032 | tf_op jit(solution)/shard_map/cthe,che->cth/dot_general | solution.py:66
  323.4 48.9 %broadcast_multiply_fusion = f32[96,256,6,128]{1,3,2,0:T(8,128)} fusion(f32[96,256,6,128]{1,3,2,0:T(8,128)} %bitcast.4, f32[96,256,6]{1,2,0:T(8,128)S(1)} %copy.59), kind=kLoop, calls=%fused_computation.21 | loop fusion | flops 18874368 | bytes 151584768 | tf_op jit(solution)/shard_map/mul | solution.py:72
  372.3 74.2 %copy.60 = f32[96,256,6,128]{3,0,2,1:T(8,128)} copy(f32[96,256,6,128]{1,3,2,0:T(8,128)} %broadcast_multiply_fusion) | data formatting | bytes 150994944 | tf_op jit(solution)/shard_map/mul | solution.py:72
  446.9 34.5 %broadcast_divide_fusion = f32[12,256,6,128]{3,0,2,1:T(8,128)} fusion(f32[12,256,6]{0,2,1:T(8,128)S(1)} %copy.61, f32[96,256,6,128]{3,0,2,1:T(8,128)} %copy.60, s32[96]{0:T(128)} %copy-done.5), kind=kOutput, calls=%fused_computation.28 | convolution fusion | flops 2720269312 | bytes 85008768 | tf_op jit(solution)/shard_map/kc,cthe->kthe/dot_general | solution.py:71
  481.4 12.1 %copy.86 = f32[12,256,6,128]{1,3,2,0:T(8,128)} copy(f32[12,256,6,128]{3,0,2,1:T(8,128)} %broadcast_divide_fusion) | data formatting | bytes 18874368
  493.5 5.0 fusion.12
  499.5 47.0 %all-reduce.3.cloned.1.call-done = bf16[256,768]{1,0:T(8,128)(2,1)} async-done(((bf16[256,768]{1,0:T(8,128)(2,1)}), bf16[256,768]{1,0:T(8,128)(2,1)}) %all-reduce.3.cloned.1.call-update) | async-done | bytes 393232 | tf_op jit(solution)/shard_map/psum | solution.py:79
  546.5 39.8 %all-gather.4.cloned.1.call-done = bf16[256,6144]{1,0:T(8,128)(2,1)} async-done(((bf16[256,768]{1,0:T(8,128)(2,1)}), bf16[256,6144]{1,0:T(8,128)(2,1)}) %all-gather.4.cloned.1.call-update) | async-done | bytes 3145744 | tf_op jit(solution)/shard_map/all_gather | solution.py:80
  586.3 3.2 convert_reduce_fusion
  589.5 7.8 %convolution_convert_fusion = bf16[256,3072]{1,0:T(8,128)(2,1)} fusion(bf16[1536,3072]{1,0:T(8,128)(2,1)} %param.20, f32[1536]{0:T(1024)S(1)} %copy-done.7, f32[256]{0:T(256)S(1)} %get-tuple-element.12, f32[256]{0:T(256)S(1)} %get-tuple-element.11, bf16[256,6144]{1,0:T(8,128)(2,1)} %all-gather.4.cloned.1.call-done, s32[]{:T(128)S(6)} %select_n.3), kind=kOutput, calls=%fused_computation.29 | convolution fusion | flops 2418671616 | bytes 11804676 | tf_op jit(solution)/shard_map/dot_general | solution.py:92
  597.4 6.5 convolution_convert_fusion.1
  604.2 23.3 %reduce-scatter.5.cloned.1.call-done = bf16[64,3072]{1,0:T(8,128)(2,1)} async-done(((bf16[256,3072]{1,0:T(8,128)(2,1)}), bf16[64,3072]{1,0:T(8,128)(2,1)}) %reduce-scatter.5.cloned.1.call-update) | async-done | bytes 393232 | tf_op jit(solution)/shard_map/reduce_scatter | solution.py:97
  627.6 3.5 fusion.20
  631.1 28.0 %reduce-scatter.3.cloned.1.call-done = bf16[64,3,768]{2,0,1:T(8,128)(2,1)} async-done(((bf16[256,3,768]{2,0,1:T(8,128)(2,1)}), bf16[64,3,768]{2,0,1:T(8,128)(2,1)}) %reduce-scatter.3.cloned.1.call-update) | async-done | bytes 294928 | tf_op jit(solution)/shard_map/reduce_scatter | solution.py:94
  660.0 9.5 %all-gather = bf16[256,1,768]{2,0,1:T(8,128)(2,1)S(1)} all-gather(bf16[64,1,768]{2,0,1:T(8,128)(2,1)S(1)} %slice.13), channel_id=2, replica_groups=mesh['chan'=4,'hid'=8] {'chan'}, dimensions={0}, use_global_device_ids=true | all-gather | bytes 491520 | tf_op jit(solution)/shard_map/all_gather | solution.py:107
  674.9 10.6 %all_gather.18 = bf16[256,768]{1,0:T(8,128)(2,1)S(1)} all-gather(bf16[64,768]{1,0:T(8,128)(2,1)S(1)} %get-tuple-element.7), channel_id=1, replica_groups=mesh['chan'=4,'hid'=8] {'chan'}, dimensions={0}, use_global_device_ids=true | all-gather | bytes 491520 | tf_op jit(solution)/shard_map/all_gather | solution.py:106
  685.6 11.0 %all_gather.17 = bf16[256,768]{1,0:T(8,128)(2,1)S(1)} all-gather(bf16[64,768]{1,0:T(8,128)(2,1)} %get-tuple-element.8), channel_id=1, replica_groups=mesh['chan'=4,'hid'=8] {'chan'}, dimensions={0}, use_global_device_ids=true | all-gather | bytes 491520 | tf_op jit(solution)/shard_map/all_gather | solution.py:105
  698.4 2.4 convolution_convert_fusion.2
  700.8 5.7 fusion.50
  708.5 62.2 %all-reduce.5.cloned.1.call-done = f32[256,1536]{1,0:T(8,128)} async-done(((f32[256,1536]{1,0:T(8,128)}), f32[256,1536]{1,0:T(8,128)}) %all-reduce.5.cloned.1.call-update) | async-done | bytes 1572880 | tf_op jit(solution)/shard_map/psum | solution.py:124
  770.6 2.7 fusion.17
  (66 shorter events, 18.2 us)
Async XLA Ops:
  6.5 699.9 %copy-start = (bf16[768,1536]{1,0:T(8,128)(2,1)S(1)}, bf16[768,1536]{1,0:T(8,128)(2,1)}, u32[]{:S(2)}) copy-start(bf16[768,1536]{1,0:T(8,128)(2,1)} %param.22) | copy-start | bytes 7077892
  6.5 539.9 %all-reduce.3.cloned.1.call-start = ((), (), s32[]{:S(2)}) async-start(), calls=%async_computation.2 | async-start | bytes 786432 | tf_op jit(solution)/shard_map/psum | solution.py:79
  7.3 0.6 copy-start.5
  255.7 23.4 %copy-start.1 = (f32[96,6,128,1]{2,3,1,0:T(1,128)S(1)}, f32[96,6,128,1]{2,3,1,0:T(1,128)}, u32[]{:S(2)}) copy-start(f32[96,6,128,1]{2,3,1,0:T(1,128)} %reshape.112) | copy-start | bytes 884740
  255.7 66.8 %copy-start.3 = (f32[96,6]{0,1:T(8,128)S(1)}, f32[96,6]{0,1:T(8,128)}, u32[]{:S(2)}) copy-start(f32[96,6]{0,1:T(8,128)} %sqrt.7) | copy-start | bytes 6916
  255.7 67.0 %copy-start.6 = (s32[96]{0:T(128)S(1)}, s32[96]{0:T(128)}, u32[]{:S(2)}) copy-start(s32[96]{0:T(128)} %copy-done.5) | copy-start | bytes 1156
  279.0 44.4 %copy-start.2 = (bf16[12,768]{1,0:T(8,128)(2,1)S(1)}, bf16[12,768]{1,0:T(8,128)(2,1)}, u32[]{:S(2)}) copy-start(bf16[12,768]{1,0:T(8,128)(2,1)} %param.16) | copy-start | bytes 55300
  446.9 142.7 %copy-start.7 = (f32[1536]{0:T(1024)S(1)}, f32[1536]{0:T(1024)}, u32[]{:S(2)}) copy-start(f32[1536]{0:T(1024)} %param.18) | copy-start | bytes 18436
  446.9 180.7 %copy-start.4 = (f32[3072]{0:T(1024)S(1)}, f32[3072]{0:T(1024)}, u32[]{:S(2)}) copy-start(f32[3072]{0:T(1024)} %param.21) | copy-start | bytes 36868
  499.5 86.9 %all-gather.4.cloned.1.call-start = ((), (), s32[]{:S(2)}) async-start(), calls=%async_computation.3 | async-start | bytes 3538944 | tf_op jit(solution)/shard_map/all_gather | solution.py:80
  546.5 81.1 %reduce-scatter.5.cloned.1.call-start = ((), (), s32[]{:S(2)}) async-start(), calls=%async_computation.5 | async-start | bytes 1966080 | tf_op jit(solution)/shard_map/reduce_scatter | solution.py:97
  597.4 61.7 %reduce-scatter.3.cloned.1.call-start = ((), (), s32[]{:S(2)}) async-start(), calls=%async_computation.4 | async-start | bytes 1474560 | tf_op jit(solution)/shard_map/reduce_scatter | solution.py:94
  603.9 96.9 %all-gather.6.cloned.1.call-start = ((), (), s32[]{:S(2)}) async-start(), calls=%async_computation.6 | async-start | bytes 1966080 | tf_op jit(solution)/shard_map/all_gather | solution.py:108
  631.1 139.6 %all-reduce.5.cloned.1.call-start = ((), (), s32[]{:S(2)}) async-start(), calls=%async_computation.7 | async-start | bytes 3145728 | tf_op jit(solution)/shard_map/psum | solution.py:124
Sparse Core Ops, SparseCore 0:
  499.6 46.8 all-reduce.2
  548.1 38.1 all-gather.3
  597.5 30.0 reduce-scatter.4
  630.3 28.7 reduce-scatter.2
  660.8 33.7 all-gather.5
  708.6 61.9 all-reduce.4
where the time goes:
time: 783 us; the launch traced here: 780 us
  matrix products  276 us (35%)
  waiting for transfers between devices  200 us (26%)
  local copies, waits for them, and re-layouts  167 us (21%)
  other arithmetic  91.4 us (12%)
  blocking collectives  31.1 us (4%)
  between operations  13.7 us (2%)
    dot_general x1, matrix products, on_device(): jnp.einsum('ctp,cpd->ctd', pixels, patch_weight, preferred_element_type=j...  171 us
    mul x1, local copies, waits for them, and re-layouts, on_device(): weight[..., None] * split  74.2 us
    mul x1, local copies, waits for them, and re-layouts, on_device(): features = jax.nn.gelu(embedded, approximate=False)  72.9 us
    psum x1, waiting for transfers between devices, on_device(): mixed = lax.psum(term, 'hid')  62.2 us
    mul x1, other arithmetic, on_device(): weight[..., None] * split  48.9 us
    psum x1, waiting for transfers between devices, on_device(): layer_sum = lax.psum(partial_value.astype(jnp.bfloat16), 'chan')  47 us
    dot_general x1, matrix products, on_device(): jnp.einsum('cthe,che->cth', normed, query, precision=lax.Precision.HIGHEST)  43.4 us
    all_gather x1, waiting for transfers between devices, on_device(): gathered = lax.all_gather(layer_sum, 'hid', axis=1, tiled=True)  39.8 us
  transfers between devices with their start and end apart: 6, of which 5 were waited for; matrix products, arithmetic and copies ran while one was open for 3% of the time, Pallas kernels for 0%

commit v1 on v0

--- a/solution.py
+++ b/solution.py
@@ -121,7 +121,7 @@
     term = jnp.dot(attended, w_out, preferred_element_type=jnp.float32) + jnp.dot(
         hidden, w_down, preferred_element_type=jnp.float32
     )
-    mixed = lax.psum(term, "hid")
+    mixed = jnp.sum(lax.all_gather(term, "hid"), axis=0)
     return (own_cols + mixed).astype(jnp.bfloat16)
 
 

time: 783 us -> 845 us (1.079)
  waiting for transfers between devices: 200 us -> 255 us
    all_gather x0 -> x1, waiting for transfers between devices: none -> 117 us  [on_device(): mixed = jnp.sum(lax.all_gather(term, 'hid'), axis=0)]
    psum x1 -> x0, waiting for transfers between devices: 62.2 us -> none  [on_device(): mixed = lax.psum(term, 'hid')]
  transfers between devices with their start and end apart: 6 -> 6, of which waited for: 5 -> 5; matrix products, arithmetic and copies ran while one was open for 3% -> 2% of each run, Pallas kernels for 0% -> 0%
where the time goes in v1:
time: 845 us; the launch traced here: 842 us
  matrix products  276 us (33%)
  waiting for transfers between devices  255 us (30%)
  local copies, waits for them, and re-layouts  167 us (20%)
  other arithmetic  98.7 us (12%)
  blocking collectives  31.1 us (4%)
  between operations  13.7 us (2%)
    dot_general x1, matrix products, on_device(): jnp.einsum('ctp,cpd->ctd', pixels, patch_weight, preferred_element_type=j...  171 us
    all_gather x1, waiting for transfers between devices, on_device(): mixed = jnp.sum(lax.all_gather(term, 'hid'), axis=0)  117 us
    mul x1, local copies, waits for them, and re-layouts, on_device(): weight[..., None] * split  74.2 us
    mul x1, local copies, waits for them, and re-layouts, on_device(): features = jax.nn.gelu(embedded, approximate=False)  72.9 us
    mul x1, other arithmetic, on_device(): weight[..., None] * split  48.9 us
    psum x1, waiting for transfers between devices, on_device(): layer_sum = lax.psum(partial_value.astype(jnp.bfloat16), 'chan')  47 us
    dot_general x1, matrix products, on_device(): jnp.einsum('cthe,che->cth', normed, query, precision=lax.Precision.HIGHEST)  43.4 us
    all_gather x1, waiting for transfers between devices, on_device(): gathered = lax.all_gather(layer_sum, 'hid', axis=1, tiled=True)  39.8 us
  transfers between devices with their start and end apart: 6, of which 5 were waited for; matrix products, arithmetic and copies ran while one was open for 2% of the time, Pallas kernels for 0%

profile of v1, /device:TPU:0, one launch (start us, length us, event | category | flops | bytes accessed | tf_op | source)
XLA Modules:
  0.0 842.1 jit_solution(14783937349802541783)
XLA Ops:
  11.8 171.0 %fusion.1 = f32[96,256,768]{2,1,0:T(8,128)} fusion(f32[96,768]{1,0:T(8,128)S(1)} %convert_element_type.64, bf16[96,256,256]{2,1,0:T(8,128)(2,1)} %param.12, bf16[96,256,768]{2,1,0:T(8,128)(2,1)} %param.13), kind=kOutput, calls=%fused_computation.2 | convolution fusion | flops 10890510336 | bytes 126124032 | tf_op jit(solution)/shard_map/ctp,cpd->ctd/dot_general | solution.py:55
  182.8 72.9 %copy.57 = f32[96,256,768]{1,2,0:T(8,128)} copy(f32[96,256,768]{2,1,0:T(8,128)} %fusion.1) | data formatting | bytes 150994944 | tf_op jit(solution)/shard_map/mul | solution.py:57
  255.7 23.3 %multiply_reduce_fusion = f32[96,256,6]{1,2,0:T(8,128)S(1)} fusion(f32[96,256,6,128]{1,3,2,0:T(8,128)} %bitcast.4), kind=kLoop, calls=%fused_computation.5 | loop fusion | flops 37601280 | bytes 76087296 | tf_op jit(solution)/shard_map/reduce_sum | solution.py:14
  279.1 43.4 %fusion.2 = f32[96,6,1,256]{3,2,1,0:T(1,128)S(1)} fusion(f32[96,6,128,1]{2,3,1,0:T(1,128)S(1)} %copy-done.1, f32[96,256,6,128]{1,3,2,0:T(8,128)} %bitcast.4, f32[96,256,6]{1,2,0:T(8,128)S(1)} %add_rsqrt_fusion), kind=kOutput, calls=%fused_computation.3 | convolution fusion | flops 245366784 | bytes 76972032 | tf_op jit(solution)/shard_map/cthe,che->cth/dot_general | solution.py:66
  323.4 48.9 %broadcast_multiply_fusion = f32[96,256,6,128]{1,3,2,0:T(8,128)} fusion(f32[96,256,6,128]{1,3,2,0:T(8,128)} %bitcast.4, f32[96,256,6]{1,2,0:T(8,128)S(1)} %copy.59), kind=kLoop, calls=%fused_computation.21 | loop fusion | flops 18874368 | bytes 151584768 | tf_op jit(solution)/shard_map/mul | solution.py:72
  372.3 74.2 %copy.60 = f32[96,256,6,128]{3,0,2,1:T(8,128)} copy(f32[96,256,6,128]{1,3,2,0:T(8,128)} %broadcast_multiply_fusion) | data formatting | bytes 150994944 | tf_op jit(solution)/shard_map/mul | solution.py:72
  446.9 34.5 %broadcast_divide_fusion = f32[12,256,6,128]{3,0,2,1:T(8,128)} fusion(f32[12,256,6]{0,2,1:T(8,128)S(1)} %copy.61, f32[96,256,6,128]{3,0,2,1:T(8,128)} %copy.60, s32[96]{0:T(128)} %copy-done.5), kind=kOutput, calls=%fused_computation.28 | convolution fusion | flops 2720269312 | bytes 85008768 | tf_op jit(solution)/shard_map/kc,cthe->kthe/dot_general | solution.py:71
  481.4 12.1 %copy.86 = f32[12,256,6,128]{1,3,2,0:T(8,128)} copy(f32[12,256,6,128]{3,0,2,1:T(8,128)} %broadcast_divide_fusion) | data formatting | bytes 18874368
  493.5 5.0 fusion.12
  499.5 47.0 %all-reduce.2.cloned.1.call-done = bf16[256,768]{1,0:T(8,128)(2,1)} async-done(((bf16[256,768]{1,0:T(8,128)(2,1)}), bf16[256,768]{1,0:T(8,128)(2,1)}) %all-reduce.2.cloned.1.call-update) | async-done | bytes 393232 | tf_op jit(solution)/shard_map/psum | solution.py:79
  546.5 39.8 %all-gather.6.cloned.1.call-done = bf16[256,6144]{1,0:T(8,128)(2,1)} async-done(((bf16[256,768]{1,0:T(8,128)(2,1)}), bf16[256,6144]{1,0:T(8,128)(2,1)}) %all-gather.6.cloned.1.call-update) | async-done | bytes 3145744 | tf_op jit(solution)/shard_map/all_gather | solution.py:80
  586.3 3.2 convert_reduce_fusion
  589.5 7.8 convolution_convert_fusion
  597.4 6.4 convolution_convert_fusion.1
  604.2 23.4 %reduce-scatter.5.cloned.1.call-done = bf16[64,3072]{1,0:T(8,128)(2,1)} async-done(((bf16[256,3072]{1,0:T(8,128)(2,1)}), bf16[64,3072]{1,0:T(8,128)(2,1)}) %reduce-scatter.5.cloned.1.call-update) | async-done | bytes 393232 | tf_op jit(solution)/shard_map/reduce_scatter | solution.py:97
  627.6 3.5 fusion.20
  631.1 28.0 %reduce-scatter.3.cloned.1.call-done = bf16[64,3,768]{2,0,1:T(8,128)(2,1)} async-done(((bf16[256,3,768]{2,0,1:T(8,128)(2,1)}), bf16[64,3,768]{2,0,1:T(8,128)(2,1)}) %reduce-scatter.3.cloned.1.call-update) | async-done | bytes 294928 | tf_op jit(solution)/shard_map/reduce_scatter | solution.py:94
  660.0 9.5 %all-gather = bf16[256,1,768]{2,0,1:T(8,128)(2,1)S(1)} all-gather(bf16[64,1,768]{2,0,1:T(8,128)(2,1)S(1)} %slice.13), channel_id=2, replica_groups=mesh['chan'=4,'hid'=8] {'chan'}, dimensions={0}, use_global_device_ids=true | all-gather | bytes 491520 | tf_op jit(solution)/shard_map/all_gather | solution.py:107
  674.8 10.4 %all_gather.24 = bf16[256,768]{1,0:T(8,128)(2,1)S(1)} all-gather(bf16[64,768]{1,0:T(8,128)(2,1)S(1)} %get-tuple-element.7), channel_id=1, replica_groups=mesh['chan'=4,'hid'=8] {'chan'}, dimensions={0}, use_global_device_ids=true | all-gather | bytes 491520 | tf_op jit(solution)/shard_map/all_gather | solution.py:106
  685.5 11.1 %all_gather.23 = bf16[256,768]{1,0:T(8,128)(2,1)S(1)} all-gather(bf16[64,768]{1,0:T(8,128)(2,1)} %get-tuple-element.8), channel_id=1, replica_groups=mesh['chan'=4,'hid'=8] {'chan'}, dimensions={0}, use_global_device_ids=true | all-gather | bytes 491520 | tf_op jit(solution)/shard_map/all_gather | solution.py:105
  700.7 5.7 fusion.50
  708.4 116.9 %all-gather.10.cloned.1.call-done = f32[2048,1536]{1,0:T(8,128)} async-done(((f32[256,1536]{1,0:T(8,128)}), f32[2048,1536]{1,0:T(8,128)}) %all-gather.10.cloned.1.call-update) | async-done | bytes 12582928 | tf_op jit(solution)/shard_map/all_gather | solution.py:124
  825.3 7.3 reduce_sum.79
  832.6 2.7 fusion.17
  (67 shorter events, 20.5 us)
Async XLA Ops:
  6.5 699.9 %copy-start = (bf16[768,1536]{1,0:T(8,128)(2,1)S(1)}, bf16[768,1536]{1,0:T(8,128)(2,1)}, u32[]{:S(2)}) copy-start(bf16[768,1536]{1,0:T(8,128)(2,1)} %param.22) | copy-start | bytes 7077892
  6.5 539.9 %all-reduce.2.cloned.1.call-start = ((), (), s32[]{:S(2)}) async-start(), calls=%async_computation.2 | async-start | bytes 786432 | tf_op jit(solution)/shard_map/psum | solution.py:79
  7.3 0.6 copy-start.5
  255.7 23.4 %copy-start.1 = (f32[96,6,128,1]{2,3,1,0:T(1,128)S(1)}, f32[96,6,128,1]{2,3,1,0:T(1,128)}, u32[]{:S(2)}) copy-start(f32[96,6,128,1]{2,3,1,0:T(1,128)} %reshape.113) | copy-start | bytes 884740
  255.7 66.8 %copy-start.3 = (f32[96,6]{0,1:T(8,128)S(1)}, f32[96,6]{0,1:T(8,128)}, u32[]{:S(2)}) copy-start(f32[96,6]{0,1:T(8,128)} %sqrt.7) | copy-start | bytes 6916
  255.7 67.0 %copy-start.6 = (s32[96]{0:T(128)S(1)}, s32[96]{0:T(128)}, u32[]{:S(2)}) copy-start(s32[96]{0:T(128)} %copy-done.5) | copy-start | bytes 1156
  279.0 44.4 %copy-start.2 = (bf16[12,768]{1,0:T(8,128)(2,1)S(1)}, bf16[12,768]{1,0:T(8,128)(2,1)}, u32[]{:S(2)}) copy-start(bf16[12,768]{1,0:T(8,128)(2,1)} %param.16) | copy-start | bytes 55300
  446.9 142.7 %copy-start.7 = (f32[1536]{0:T(1024)S(1)}, f32[1536]{0:T(1024)}, u32[]{:S(2)}) copy-start(f32[1536]{0:T(1024)} %param.18) | copy-start | bytes 18436
  446.9 180.7 %copy-start.4 = (f32[3072]{0:T(1024)S(1)}, f32[3072]{0:T(1024)}, u32[]{:S(2)}) copy-start(f32[3072]{0:T(1024)} %param.21) | copy-start | bytes 36868
  499.5 86.9 %all-gather.6.cloned.1.call-start = ((), (), s32[]{:S(2)}) async-start(), calls=%async_computation.3 | async-start | bytes 3538944 | tf_op jit(solution)/shard_map/all_gather | solution.py:80
  546.5 81.1 %reduce-scatter.5.cloned.1.call-start = ((), (), s32[]{:S(2)}) async-start(), calls=%async_computation.5 | async-start | bytes 1966080 | tf_op jit(solution)/shard_map/reduce_scatter | solution.py:97
  597.4 61.7 %reduce-scatter.3.cloned.1.call-start = ((), (), s32[]{:S(2)}) async-start(), calls=%async_computation.4 | async-start | bytes 1474560 | tf_op jit(solution)/shard_map/reduce_scatter | solution.py:94
  603.9 96.8 %all-gather.8.cloned.1.call-start = ((), (), s32[]{:S(2)}) async-start(), calls=%async_computation.6 | async-start | bytes 1966080 | tf_op jit(solution)/shard_map/all_gather | solution.py:108
  631.1 194.2 %all-gather.10.cloned.1.call-start = ((), (), s32[]{:S(2)}) async-start(), calls=%async_computation.7 | async-start | bytes 14155776 | tf_op jit(solution)/shard_map/all_gather | solution.py:124
Sparse Core Ops, SparseCore 0:
  499.6 46.8 all-reduce.1
  548.1 38.1 all-gather.5
  597.5 30.0 reduce-scatter.4
  630.4 28.7 reduce-scatter.2
  660.8 33.6 all-gather.7
  708.5 116.7 all-gather.9
